TPU v7x, 512 devices: a whole 4x8x8 slice. The times are simulated.
512 devices in a mesh: blk: 16 (over y, z_lo), wide: 32 (over x, z_hi, core).
Axes of the slice: x: 4, y: 8, z: 8 (z_hi: 4, z_lo: 2; z = z_hi * 2 + z_lo), core: 2. Of those that a mesh axis runs over, the one named last changes fastest.
Arguments:
- tokens: bfloat16 [24576, 128], P(('blk', 'wide')), may hold values from -11 to 11
- centroids: bfloat16 [131072, 128], P('blk'), may hold values from -7 to 7
- row_ids: int32 [512, 16, 32], P(('blk', 'wide')), may hold values from 0 to 47
- alt_ids: int32 [512, 16, 32], P(('blk', 'wide')), may hold values from 0 to 8191
- counts: int32 [512, 16], P(('blk', 'wide')), may hold values from 1 to 32, as said below
Outputs:
- row_duals: float32 [24576], P(('blk', 'wide'))
- col_duals: float32 [131072], P('blk')
- residuals: float32 [512, 16, 32, 128], P(('blk', 'wide'))
Inputs may be any that keep to these rules, and one draw needn't show every extreme that they name: `row_ids`: slot (d, b, c) names row d * 48 + value. `alt_ids`: slot (d, b, c) names centroid b * 8192 + value. The first counts[d, b] slots of device d toward owner b are live; one owner, the same on every device, gets 32 live slots from every device.
All inputs are finite; a program needn't handle non-finite values.
Results may differ from a plain program's by a relative error of at most 0.0003.
Values may be sent and summed in bfloat16 or wider, within the bound.
No kernel may reach another device: no remote copies, remote signals or barrier semaphores. Data moves between devices by JAX's collectives and lax.ppermute only.
A program may use at most 64 MiB of HBM per device.

v0:
```python
import math
import jax
import jax.numpy as jnp
from jax import lax
from jax.sharding import PartitionSpec as P

score_gain = 3.0


def local(tokens, centroids, row_ids, alt_ids, counts):
    scaling = score_gain / math.sqrt(tokens.shape[1])
    blk_count = lax.axis_size("blk")
    wide_count = lax.axis_size("wide")
    position = lax.axis_index("blk")
    tok_dev = tokens.shape[0]
    slab = centroids.shape[0]
    all_cols = slab * blk_count
    all_rows = tok_dev * blk_count * wide_count
    gathered = lax.all_gather(tokens, "blk", axis=0, tiled=True)
    group_rows = gathered.shape[0]
    block_cols = math.gcd(slab, 1024)
    col_blocks = centroids.reshape(slab // block_cols, block_cols, centroids.shape[1])

    def block_scores(centre_block):
        return (
            jnp.einsum("rd,kd->rk", gathered, centre_block, preferred_element_type=jnp.float32)
            * scaling
        )

    def online_step(carry, centre_block):
        running_peak, running_total = carry
        scores = block_scores(centre_block)
        new_peak = jnp.maximum(running_peak, jnp.max(scores, axis=1))
        new_total = running_total * jnp.exp(running_peak - new_peak) + jnp.sum(
            jnp.exp(scores - new_peak[:, None]), axis=1
        )
        return ((new_peak, new_total), None)

    initial = (
        jnp.full((group_rows,), -jnp.inf, jnp.float32),
        jnp.zeros((group_rows,), jnp.float32),
    )
    (local_peak, local_total), unused = lax.scan(online_step, initial, col_blocks)
    peak_score = lax.pmax(local_peak, "blk")
    totals = lax.psum(local_total * jnp.exp(local_peak - peak_score), "blk")
    row_group = math.log(all_cols) - (peak_score + jnp.log(totals))

    def block_mass(centre_block):
        scores = block_scores(centre_block)
        return jnp.sum(jnp.exp(scores + row_group[:, None]), axis=0)

    partial_mass = lax.map(block_mass, col_blocks).reshape(slab)
    col_duals = math.log(all_rows) - jnp.log(lax.psum(partial_mass, "wide"))
    row_duals = lax.dynamic_slice_in_dim(row_group, position * tok_dev, tok_dev)
    request_rows = row_ids[0]
    request_cols = alt_ids[0]
    capacity = request_rows.shape[1]
    live = (jnp.arange(capacity, dtype=jnp.int32)[None, :] < counts[0][:, None]).astype(jnp.int32)
    source_base = jnp.arange(blk_count, dtype=jnp.int32)[:, None] * tok_dev
    asked_rows = lax.all_to_all(request_rows, "blk", split_axis=0, concat_axis=0, tiled=True)
    asked_cols = lax.all_to_all(request_cols, "blk", split_axis=0, concat_axis=0, tiled=True)
    asked_live = lax.all_to_all(live, "blk", split_axis=0, concat_axis=0, tiled=True)
    rows_index = source_base + asked_rows
    picked = gathered[rows_index].astype(jnp.float32)
    centres = centroids[asked_cols].astype(jnp.float32)
    pair_scores = jnp.sum(picked * centres, axis=-1) * scaling
    picked, centres, weights = (
        picked,
        centres,
        jnp.exp(pair_scores + row_group[rows_index] + col_duals[asked_cols]),
    )
    weights = weights * asked_live.astype(jnp.float32)
    result = weights[..., None] * (picked - centres)
    residuals = lax.all_to_all(result, "blk", split_axis=0, concat_axis=0, tiled=True)
    return (row_duals, col_duals, residuals[None])


def solution(mesh):
    in_specs = (
        P(("blk", "wide"), None),
        P("blk", None),
        P(("blk", "wide"), None, None),
        P(("blk", "wide"), None, None),
        P(("blk", "wide"), None),
    )
    out_specs = (P(("blk", "wide")), P("blk"), P(("blk", "wide"), None, None, None))
    return jax.shard_map(local, mesh=mesh, in_specs=in_specs, out_specs=out_specs, check_vma=False)
```

profile of v0, /device:TPU:8, one launch (start us, length us, event | category | flops | bytes accessed | tf_op | source)
XLA Modules:
  0.0 324.0 jit_solution(13096027828668826560)
XLA Ops:
  0.6 9.4 %all-to-all-start = ((s32[16,1,32]{2,1,0:T(1,128)}), s32[16,1,32]{2,1,0:T(1,128)S(1)}, u32[]{:S(2)}, u32[]{:S(2)}) async-start(s32[16,1,32]{2,1,0:T(1,128)} %bitcast.48), calls=%async_computation | async-start | bytes 16384 | tf_op jit(solution)/shard_map/all_to_all | solution.py:60
  10.0 32.4 %all_gather.3 = bf16[768,128]{1,0:T(8,128)(2,1)S(1)} all-gather(bf16[48,128]{1,0:T(8,128)(2,1)} %param.9), channel_id=1, replica_groups=mesh['blk'=16,'wide'=32] {'blk'}, dimensions={0}, use_global_device_ids=true | all-gather | bytes 208896 | tf_op jit(solution)/shard_map/all_gather | solution.py:19
  42.4 17.3 %while.24 = (s32[]{:T(128)}, f32[768]{0:T(1024)S(1)}, f32[768]{0:T(1024)S(1)}, bf16[8,1024,128]{2,1,0:T(8,128)(2,1)}, bf16[768,128]{1,0:T(8,128)(2,1)S(1)}, /*index=5*/s32[]{:T(128)}, s32[]{:T(128)}) while((s32[]{:T(128)}, f32[768]{0:T(1024)S(1)}, f32[768]{0:T(1024)S(1)}, bf16[8,1024,128]{2,1,0:T(8,128)(2,1)}, ...), condition=%wide.region_3.4_spmd.clone, body=%wide.region_0.3_spmd.clone.sunk | while | flops 205262592 | bytes 6790244 | solution.py:43
  42.4 1.5 multiply_reduce_fusion.2
  44.0 0.6 exponential_reduce_fusion.5
  44.6 1.5 multiply_reduce_fusion.2
  46.1 0.6 exponential_reduce_fusion.5
  46.7 1.5 multiply_reduce_fusion.2
  48.3 0.6 exponential_reduce_fusion.5
  48.9 1.5 multiply_reduce_fusion.2
  50.4 0.6 exponential_reduce_fusion.5
  51.0 1.5 multiply_reduce_fusion.2
  52.6 0.6 exponential_reduce_fusion.5
  53.2 1.5 multiply_reduce_fusion.2
  54.8 0.6 exponential_reduce_fusion.5
  55.4 1.5 multiply_reduce_fusion.2
  56.9 0.6 exponential_reduce_fusion.5
  57.5 1.5 multiply_reduce_fusion.2
  59.1 0.6 exponential_reduce_fusion.5
  59.7 30.6 %pmax.7 = f32[768]{0:T(1024)S(1)} all-reduce(f32[768]{0:T(1024)S(1)} %get-tuple-element.58), channel_id=1, replica_groups=mesh['blk'=16,'wide'=32] {'blk'}, use_global_device_ids=true, to_apply=%region_4.5 | all-reduce | flops 768 | bytes 6144 | tf_op jit(solution)/shard_map/pmax | solution.py:44
  90.3 32.6 %psum.14 = f32[768]{0:T(1024)S(1)} all-reduce(f32[768]{0:T(1024)S(1)} %exponential_multiply_fusion), channel_id=1, replica_groups=mesh['blk'=16,'wide'=32] {'blk'}, use_global_device_ids=true, to_apply=%region_5.6 | all-reduce | flops 768 | bytes 6144 | tf_op jit(solution)/shard_map/psum | solution.py:45
  123.0 14.5 %while.23 = (s32[]{:T(128)}, f32[8,1024]{1,0:T(8,128)S(1)}, bf16[8,1024,128]{2,1,0:T(8,128)(2,1)}, bf16[768,128]{1,0:T(8,128)(2,1)S(1)}, f32[768]{0:T(1024)S(1)}, /*index=5*/s32[]{:T(128)}, s32[]{:T(128)}) while((s32[]{:T(128)}, f32[8,1024]{1,0:T(8,128)S(1)}, bf16[8,1024,128]{2,1,0:T(8,128)(2,1)}, bf16[768,128]{1,0:T(8,128)(2,1)S(1)}, ...), condition=%wide.region_8.9_spmd, body=%wide.region_6.8_spmd.sunk | while | flops 203684864 | bytes 474205 | solution.py:52
  123.0 1.7 exponential_reduce_fusion.4
  124.6 0.1 dynamic_update_slice.5
  124.8 1.7 exponential_reduce_fusion.4
  126.5 0.1 dynamic_update_slice.5
  126.6 1.7 exponential_reduce_fusion.4
  128.3 0.1 dynamic_update_slice.5
  128.4 1.7 exponential_reduce_fusion.4
  130.1 0.1 dynamic_update_slice.5
  130.2 1.7 exponential_reduce_fusion.4
  131.9 0.1 dynamic_update_slice.5
  132.0 1.7 exponential_reduce_fusion.4
  133.7 0.1 dynamic_update_slice.5
  133.8 1.7 exponential_reduce_fusion.4
  135.5 0.1 dynamic_update_slice.5
  135.6 1.7 exponential_reduce_fusion.4
  137.3 0.1 dynamic_update_slice.5
  137.5 142.6 %psum.15 = f32[8192]{0:T(1024)S(1)} all-reduce(f32[8192]{0:T(1024)S(1)} %bitcast.42), channel_id=1, replica_groups=mesh['blk'=16,'wide'=32] {'wide'}, use_global_device_ids=true, to_apply=%region_9.10 | all-reduce | flops 8192 | bytes 65536 | tf_op jit(solution)/shard_map/psum | solution.py:53
  280.1 0.0 copy-start
  280.1 0.0 copy-done.2
  280.1 0.7 compare_convert_fusion
  280.8 0.0 all-to-all-done
  280.8 7.3 %all-to-all-start.1 = ((s32[16,1,32]{2,1,0:T(1,128)}), s32[16,1,32]{2,1,0:T(1,128)S(1)}, u32[]{:S(2)}, u32[]{:S(2)}) async-start(s32[16,1,32]{2,1,0:T(1,128)} %bitcast.5), calls=%async_computation.1 | async-start | bytes 16384 | tf_op jit(solution)/shard_map/all_to_all | solution.py:61
  288.1 0.1 compare_select_fusion.1
  288.2 0.1 reshape.157
  288.3 1.3 gather_fusion
  289.6 0.0 copy-start.1
  289.6 2.3 gather_fusion.2
  291.9 3.3 %all-to-all-done.1 = s32[16,1,32]{2,1,0:T(1,128)S(1)} async-done(((s32[16,1,32]{2,1,0:T(1,128)}), s32[16,1,32]{2,1,0:T(1,128)S(1)}, u32[]{:S(2)}, u32[]{:S(2)}) %all-to-all-start.1) | async-done | bytes 2080 | tf_op jit(solution)/shard_map/all_to_all | solution.py:61
  295.2 4.9 %all-to-all-start.2 = ((s32[16,1,32]{2,1,0:T(1,128)}), s32[16,1,32]{2,1,0:T(1,128)S(1)}, u32[]{:S(2)}, u32[]{:S(2)}) async-start(s32[16,1,32]{2,1,0:T(1,128)} %compare_convert_fusion), calls=%async_computation.2 | async-start | bytes 16384 | tf_op jit(solution)/shard_map/all_to_all | solution.py:62
  300.1 0.1 reshape.165
  300.2 0.0 copy-done.1
  300.2 1.3 gather_fusion.1
  301.5 0.0 copy-done
  301.5 3.1 gather_fusion.3
  304.7 0.1 fusion.8
  304.8 0.1 reshape.200
  304.9 2.2 all-to-all-done.2
  307.2 0.8 broadcast_multiply_fusion
  308.0 5.9 %all-to-all-start.3 = ((f32[16,32,128]{2,1,0:T(8,128)}), f32[16,32,128]{2,1,0:T(8,128)S(1)}, u32[]{:S(2)}, u32[]{:S(2)}) async-start(f32[16,32,128]{2,1,0:T(8,128)} %broadcast_multiply_fusion), calls=%async_computation.3 | async-start | bytes 524288 | tf_op jit(solution)/shard_map/all_to_all | solution.py:74
  313.9 0.6 dynamic_slice.10
  314.5 8.8 %all-to-all-done.3 = f32[16,32,128]{2,1,0:T(8,128)S(1)} async-done(((f32[16,32,128]{2,1,0:T(8,128)}), f32[16,32,128]{2,1,0:T(8,128)S(1)}, u32[]{:S(2)}, u32[]{:S(2)}) %all-to-all-start.3) | async-done | bytes 262176 | tf_op jit(solution)/shard_map/all_to_all | solution.py:74
  323.3 0.7 copy.28
  (39 shorter events, 0.2 us)
Async XLA Ops:
  0.6 280.2 %all-to-all-start = ((s32[16,1,32]{2,1,0:T(1,128)}), s32[16,1,32]{2,1,0:T(1,128)S(1)}, u32[]{:S(2)}, u32[]{:S(2)}) async-start(s32[16,1,32]{2,1,0:T(1,128)} %bitcast.48), calls=%async_computation | async-start | bytes 16384 | tf_op jit(solution)/shard_map/all_to_all | solution.py:60
  123.0 157.2 %copy-start.2 = (s32[1,16]{1,0:T(1,128)S(1)}, s32[1,16]{1,0:T(1,128)}, u32[]{:S(2)}) copy-start(s32[1,16]{1,0:T(1,128)} %param.13) | copy-start | bytes 196
  280.1 21.4 %copy-start = (f32[8192]{0:T(1024)}, f32[8192]{0:T(1024)S(1)}, u32[]{:S(2)}) copy-start(f32[8192]{0:T(1024)S(1)} %log_subtract_fusion) | copy-start | bytes 98308
  280.8 14.4 %all-to-all-start.1 = ((s32[16,1,32]{2,1,0:T(1,128)}), s32[16,1,32]{2,1,0:T(1,128)S(1)}, u32[]{:S(2)}, u32[]{:S(2)}) async-start(s32[16,1,32]{2,1,0:T(1,128)} %bitcast.5), calls=%async_computation.1 | async-start | bytes 16384 | tf_op jit(solution)/shard_map/all_to_all | solution.py:61
  289.6 10.6 %copy-start.1 = (bf16[8,1024,128]{2,1,0:T(8,128)(2,1)S(1)}, bf16[8,1024,128]{2,1,0:T(8,128)(2,1)}, u32[]{:S(2)}) copy-start(bf16[8,1024,128]{2,1,0:T(8,128)(2,1)} %get-tuple-element.221) | copy-start | bytes 6291460
  295.2 12.0 %all-to-all-start.2 = ((s32[16,1,32]{2,1,0:T(1,128)}), s32[16,1,32]{2,1,0:T(1,128)S(1)}, u32[]{:S(2)}, u32[]{:S(2)}) async-start(s32[16,1,32]{2,1,0:T(1,128)} %compare_convert_fusion), calls=%async_computation.2 | async-start | bytes 16384 | tf_op jit(solution)/shard_map/all_to_all | solution.py:62
  308.0 15.3 %all-to-all-start.3 = ((f32[16,32,128]{2,1,0:T(8,128)}), f32[16,32,128]{2,1,0:T(8,128)S(1)}, u32[]{:S(2)}, u32[]{:S(2)}) async-start(f32[16,32,128]{2,1,0:T(8,128)} %broadcast_multiply_fusion), calls=%async_computation.3 | async-start | bytes 524288 | tf_op jit(solution)/shard_map/all_to_all | solution.py:74
where the time goes:
time: 325 us; the launch traced here: 324 us
  blocking collectives  238 us (73%)
  starting transfers between devices  27.5 us (8%)
  matrix products  25.6 us (8%)
  waiting for transfers between devices  14.3 us (4%)
  local copies, waits for them, and re-layouts  10.5 us (3%)
  other arithmetic  6.47 us (2%)
    psum x1, blocking collectives, local(): col_duals = math.log(all_rows) - jnp.log(lax.psum(partial_mass, 'wide'))  143 us
    psum x1, blocking collectives, local(): totals = lax.psum(local_total * jnp.exp(local_peak - peak_score), 'blk')  32.6 us
    all_gather x1, blocking collectives, local(): gathered = lax.all_gather(tokens, 'blk', axis=0, tiled=True)  32.4 us
    pmax x1, blocking collectives, local(): peak_score = lax.pmax(local_peak, 'blk')  30.6 us
    dot_general x16, matrix products, block_scores(): jnp.einsum('rd,kd->rk', gathered, centre_block, preferred_element_type=jn...  25.6 us
    all_to_all x1, starting transfers between devices, local(): lax.all_to_all(request_rows, 'blk', split_axis=0, concat_axis=0, tiled=True)  9.38 us
    all_to_all x1, waiting for transfers between devices, local(): lax.all_to_all(result, 'blk', split_axis=0, concat_axis=0, tiled=True)  8.82 us
    all_to_all x1, starting transfers between devices, local(): lax.all_to_all(request_cols, 'blk', split_axis=0, concat_axis=0, tiled=True)  7.3 us
  transfers between devices with their start and end apart: 4, of which 3 were waited for; matrix products, arithmetic and copies ran while one was open for 13% of the time, Pallas kernels for 0%

commit v1 on v0

--- a/solution.py
+++ b/solution.py
@@ -50,7 +50,7 @@
         return jnp.sum(jnp.exp(scores + row_group[:, None]), axis=0)
 
     partial_mass = lax.map(block_mass, col_blocks).reshape(slab)
-    col_duals = math.log(all_rows) - jnp.log(lax.psum(partial_mass, "wide"))
+    col_duals = math.log(all_rows) - jnp.log(jnp.sum(lax.all_gather(partial_mass, "wide"), axis=0))
     row_duals = lax.dynamic_slice_in_dim(row_group, position * tok_dev, tok_dev)
     request_rows = row_ids[0]
     request_cols = alt_ids[0]

time: 325 us -> 231 us (0.71)
  the two profiles are of different devices: /device:TPU:8 before, /device:TPU:1 now
where the time goes in v1:
time: 231 us
  blocking collectives  78.9 us (34%)
  waiting for transfers between devices  74.1 us (32%)
  matrix products  25.5 us (11%)
  starting transfers between devices  17.7 us (8%)
  between operations  14.2 us (6%)
  local copies, waits for them, and re-layouts  11.2 us (5%)
  other arithmetic  8.39 us (4%)
    all_gather x1, waiting for transfers between devices, local(): lax.all_gather(partial_mass, 'wide')  47.8 us
    all_gather x1, blocking collectives, local(): gathered = lax.all_gather(tokens, 'blk', axis=0, tiled=True)  30 us
    dot_general x16, matrix products, block_scores(): jnp.einsum('rd,kd->rk', gathered, centre_block, preferred_element_type=jn...  25.5 us
    psum x1, blocking collectives, local(): totals = lax.psum(local_total * jnp.exp(local_peak - peak_score), 'blk')  25.2 us
    pmax x1, blocking collectives, local(): peak_score = lax.pmax(local_peak, 'blk')  23.7 us
    all_to_all x1, waiting for transfers between devices, local(): lax.all_to_all(result, 'blk', split_axis=0, concat_axis=0, tiled=True)  10.6 us
    all_to_all x1, waiting for transfers between devices, local(): lax.all_to_all(request_rows, 'blk', split_axis=0, concat_axis=0, tiled=True)  7.12 us
    all_to_all x1, waiting for transfers between devices, local(): lax.all_to_all(request_cols, 'blk', split_axis=0, concat_axis=0, tiled=True)  6.58 us
  transfers between devices with their start and end apart: 5, of which 5 were waited for; matrix products, arithmetic and copies ran while one was open for 3% of the time, Pallas kernels for 0%

profile of v1, /device:TPU:1, one launch (start us, length us, event | category | flops | bytes accessed | tf_op | source)
XLA Modules:
  0.0 230.5 jit_solution(13576784273176919774)
XLA Ops:
  7.2 0.0 all-gather.3.cloned.1.call-start
  7.2 30.0 %all_gather.6 = bf16[768,128]{1,0:T(8,128)(2,1)S(1)} all-gather(bf16[48,128]{1,0:T(8,128)(2,1)} %param.9), channel_id=1, replica_groups=mesh['blk'=16,'wide'=32] {'blk'}, dimensions={0}, use_global_device_ids=true | all-gather | bytes 208896 | tf_op jit(solution)/shard_map/all_gather | solution.py:19
  37.2 17.2 %while.24 = (s32[]{:T(128)}, f32[768]{0:T(1024)S(1)}, f32[768]{0:T(1024)S(1)}, bf16[8,1024,128]{2,1,0:T(8,128)(2,1)}, bf16[768,128]{1,0:T(8,128)(2,1)S(1)}, /*index=5*/s32[]{:T(128)}, s32[]{:T(128)}) while((s32[]{:T(128)}, f32[768]{0:T(1024)S(1)}, f32[768]{0:T(1024)S(1)}, bf16[8,1024,128]{2,1,0:T(8,128)(2,1)}, ...), condition=%wide.region_3.4_spmd.clone, body=%wide.region_0.3_spmd.clone.sunk | while | flops 205262592 | bytes 6790244 | solution.py:43
  37.2 1.5 multiply_reduce_fusion.2
  38.8 0.6 exponential_reduce_fusion.5
  39.4 1.5 multiply_reduce_fusion.2
  40.9 0.6 exponential_reduce_fusion.5
  41.5 1.5 multiply_reduce_fusion.2
  43.1 0.6 exponential_reduce_fusion.5
  43.7 1.5 multiply_reduce_fusion.2
  45.2 0.6 exponential_reduce_fusion.5
  45.8 1.5 multiply_reduce_fusion.2
  47.4 0.6 exponential_reduce_fusion.5
  48.0 1.5 multiply_reduce_fusion.2
  49.5 0.6 exponential_reduce_fusion.5
  50.1 1.5 multiply_reduce_fusion.2
  51.7 0.6 exponential_reduce_fusion.5
  52.3 1.5 multiply_reduce_fusion.2
  53.9 0.6 exponential_reduce_fusion.5
  54.4 23.7 %pmax.7 = f32[768]{0:T(1024)S(1)} all-reduce(f32[768]{0:T(1024)S(1)} %get-tuple-element.58), channel_id=1, replica_groups=mesh['blk'=16,'wide'=32] {'blk'}, use_global_device_ids=true, to_apply=%region_4.5 | all-reduce | flops 768 | bytes 6144 | tf_op jit(solution)/shard_map/pmax | solution.py:44
  78.1 25.2 %psum.7 = f32[768]{0:T(1024)S(1)} all-reduce(f32[768]{0:T(1024)S(1)} %exponential_multiply_fusion), channel_id=1, replica_groups=mesh['blk'=16,'wide'=32] {'blk'}, use_global_device_ids=true, to_apply=%region_5.6 | all-reduce | flops 768 | bytes 6144 | tf_op jit(solution)/shard_map/psum | solution.py:45
  103.4 14.4 %while.23 = (s32[]{:T(128)}, f32[8,1024]{1,0:T(8,128)S(1)}, bf16[8,1024,128]{2,1,0:T(8,128)(2,1)}, bf16[768,128]{1,0:T(8,128)(2,1)S(1)}, f32[768]{0:T(1024)S(1)}, /*index=5*/s32[]{:T(128)}, s32[]{:T(128)}) while((s32[]{:T(128)}, f32[8,1024]{1,0:T(8,128)S(1)}, bf16[8,1024,128]{2,1,0:T(8,128)(2,1)}, bf16[768,128]{1,0:T(8,128)(2,1)S(1)}, ...), condition=%wide.region_8.9_spmd, body=%wide.region_6.8_spmd.sunk | while | flops 203684864 | bytes 474205 | solution.py:52
  103.4 1.7 exponential_reduce_fusion.4
  105.0 0.1 dynamic_update_slice.5
  105.2 1.7 exponential_reduce_fusion.4
  106.8 0.1 dynamic_update_slice.5
  107.0 1.7 exponential_reduce_fusion.4
  108.6 0.1 dynamic_update_slice.5
  108.8 1.7 exponential_reduce_fusion.4
  110.4 0.1 dynamic_update_slice.5
  110.6 1.7 exponential_reduce_fusion.4
  112.2 0.1 dynamic_update_slice.5
  112.4 1.7 exponential_reduce_fusion.4
  114.0 0.1 dynamic_update_slice.5
  114.2 1.7 exponential_reduce_fusion.4
  115.8 0.1 dynamic_update_slice.5
  116.0 1.7 exponential_reduce_fusion.4
  117.6 0.1 dynamic_update_slice.5
  117.8 0.7 reshape.194
  118.4 0.0 all-gather.3.cloned.1.call-update
  118.4 4.1 %all-to-all-start.1 = ((s32[16,1,32]{2,1,0:T(1,128)}), s32[16,1,32]{2,1,0:T(1,128)S(1)}, u32[]{:S(2)}, u32[]{:S(2)}) async-start(s32[16,1,32]{2,1,0:T(1,128)} %bitcast.5), calls=%async_computation.1 | async-start | bytes 16384 | tf_op jit(solution)/shard_map/all_to_all | solution.py:61
  122.6 0.7 compare_convert_fusion
  123.3 6.6 %all-to-all-done.1 = s32[16,1,32]{2,1,0:T(1,128)S(1)} async-done(((s32[16,1,32]{2,1,0:T(1,128)}), s32[16,1,32]{2,1,0:T(1,128)S(1)}, u32[]{:S(2)}, u32[]{:S(2)}) %all-to-all-start.1) | async-done | bytes 2080 | tf_op jit(solution)/shard_map/all_to_all | solution.py:61
  129.8 3.5 %all-to-all-start = ((s32[16,1,32]{2,1,0:T(1,128)}), s32[16,1,32]{2,1,0:T(1,128)S(1)}, u32[]{:S(2)}, u32[]{:S(2)}) async-start(s32[16,1,32]{2,1,0:T(1,128)} %bitcast.3), calls=%async_computation | async-start | bytes 16384 | tf_op jit(solution)/shard_map/all_to_all | solution.py:60
  133.3 0.1 reshape.161
  133.4 7.1 %all-to-all-done = s32[16,1,32]{2,1,0:T(1,128)S(1)} async-done(((s32[16,1,32]{2,1,0:T(1,128)}), s32[16,1,32]{2,1,0:T(1,128)S(1)}, u32[]{:S(2)}, u32[]{:S(2)}) %all-to-all-start) | async-done | bytes 2080 | tf_op jit(solution)/shard_map/all_to_all | solution.py:60
  140.5 3.5 %all-to-all-start.2 = ((s32[16,1,32]{2,1,0:T(1,128)}), s32[16,1,32]{2,1,0:T(1,128)S(1)}, u32[]{:S(2)}, u32[]{:S(2)}) async-start(s32[16,1,32]{2,1,0:T(1,128)} %compare_convert_fusion), calls=%async_computation.2 | async-start | bytes 16384 | tf_op jit(solution)/shard_map/all_to_all | solution.py:62
  144.0 0.1 compare_select_fusion.1
  144.1 0.1 reshape.153
  144.2 1.3 gather_fusion
  145.5 2.3 gather_fusion.2
  147.9 1.3 gather_fusion.1
  149.2 2.0 all-to-all-done.2
  151.2 0.1 fusion.8
  151.4 47.8 %all-gather.3.cloned.1.call-done = f32[32,1,8192]{2,1,0:T(1,128)} async-done(((f32[1,1,8192]{2,1,0:T(1,128)}), f32[32,1,8192]{2,1,0:T(1,128)}) %all-gather.3.cloned.1.call-update) | async-done | bytes 1048592 | tf_op jit(solution)/shard_map/all_gather | solution.py:53
  199.2 1.9 reduce_sum.36
  201.1 0.0 copy-start
  201.1 3.1 %gather_fusion.3 = f32[512]{0:T(512)S(1)} fusion(f32[8192]{0:T(1024)S(1)} %log_subtract_fusion, s32[1024]{0:T(1024)S(1)} %pad_clamp_fusion), kind=kCustom, calls=%fused_computation.3 | custom fusion | bytes 6144 | tf_op jit(solution)/shard_map/gather | solution.py:70
  204.3 0.1 reshape.199
  204.4 0.8 broadcast_multiply_fusion
  205.2 6.6 %all-to-all-start.3 = ((f32[16,32,128]{2,1,0:T(8,128)}), f32[16,32,128]{2,1,0:T(8,128)S(1)}, u32[]{:S(2)}, u32[]{:S(2)}) async-start(f32[16,32,128]{2,1,0:T(8,128)} %broadcast_multiply_fusion), calls=%async_computation.3 | async-start | bytes 524288 | tf_op jit(solution)/shard_map/all_to_all | solution.py:74
  211.8 0.6 dynamic_slice.10
  212.4 10.6 %all-to-all-done.3 = f32[16,32,128]{2,1,0:T(8,128)S(1)} async-done(((f32[16,32,128]{2,1,0:T(8,128)}), f32[16,32,128]{2,1,0:T(8,128)S(1)}, u32[]{:S(2)}, u32[]{:S(2)}) %all-to-all-start.3) | async-done | bytes 262176 | tf_op jit(solution)/shard_map/all_to_all | solution.py:74
  223.0 0.7 copy.25
  (42 shorter events, 0.2 us)
Async XLA Ops:
  7.2 192.0 %all-gather.3.cloned.1.call-start = ((), (), s32[]{:S(2)}) async-start(), calls=%async_computation.4 | async-start | bytes 1081344 | tf_op jit(solution)/shard_map/all_gather | solution.py:53
  103.4 19.2 %copy-start.2 = (s32[1,16]{1,0:T(1,128)S(1)}, s32[1,16]{1,0:T(1,128)}, u32[]{:S(2)}) copy-start(s32[1,16]{1,0:T(1,128)} %param.13) | copy-start | bytes 196
  118.4 11.4 %all-to-all-start.1 = ((s32[16,1,32]{2,1,0:T(1,128)}), s32[16,1,32]{2,1,0:T(1,128)S(1)}, u32[]{:S(2)}, u32[]{:S(2)}) async-start(s32[16,1,32]{2,1,0:T(1,128)} %bitcast.5), calls=%async_computation.1 | async-start | bytes 16384 | tf_op jit(solution)/shard_map/all_to_all | solution.py:61
  129.8 10.7 %all-to-all-start = ((s32[16,1,32]{2,1,0:T(1,128)}), s32[16,1,32]{2,1,0:T(1,128)S(1)}, u32[]{:S(2)}, u32[]{:S(2)}) async-start(s32[16,1,32]{2,1,0:T(1,128)} %bitcast.3), calls=%async_computation | async-start | bytes 16384 | tf_op jit(solution)/shard_map/all_to_all | solution.py:60
  140.5 10.7 %all-to-all-start.2 = ((s32[16,1,32]{2,1,0:T(1,128)}), s32[16,1,32]{2,1,0:T(1,128)S(1)}, u32[]{:S(2)}, u32[]{:S(2)}) async-start(s32[16,1,32]{2,1,0:T(1,128)} %compare_convert_fusion), calls=%async_computation.2 | async-start | bytes 16384 | tf_op jit(solution)/shard_map/all_to_all | solution.py:62
  145.5 2.3 %copy-start.1 = (bf16[8,1024,128]{2,1,0:T(8,128)(2,1)S(1)}, bf16[8,1024,128]{2,1,0:T(8,128)(2,1)}, u32[]{:S(2)}) copy-start(bf16[8,1024,128]{2,1,0:T(8,128)(2,1)} %get-tuple-element.222) | copy-start | bytes 6291460
  201.1 3.2 %copy-start = (f32[8192]{0:T(1024)}, f32[8192]{0:T(1024)S(1)}, u32[]{:S(2)}) copy-start(f32[8192]{0:T(1024)S(1)} %log_subtract_fusion) | copy-start | bytes 98308
  205.2 17.7 %all-to-all-start.3 = ((f32[16,32,128]{2,1,0:T(8,128)}), f32[16,32,128]{2,1,0:T(8,128)S(1)}, u32[]{:S(2)}, u32[]{:S(2)}) async-start(f32[16,32,128]{2,1,0:T(8,128)} %broadcast_multiply_fusion), calls=%async_computation.3 | async-start | bytes 524288 | tf_op jit(solution)/shard_map/all_to_all | solution.py:74
Sparse Core Ops, SparseCore 0:
  118.6 80.5 all-gather.2
